TPU v7x, 256 devices: a whole 4x4x8 slice. The times are simulated.
256 devices in a mesh: group: 8 (over x, core), batch: 32 (over z, y).
Axes of the slice: x: 4, y: 4, z: 8, core: 2. Of those that a mesh axis runs over, the one named last changes fastest.
Arguments:
- panel_alleles: int32 [64, 131072], P('group', 'batch'), may hold values 0 or 1
- recomb_rates: float32 [64], P('group'), may hold values from 0.001 to 0.3
- genotypes: int32 [2, 64], P(None, 'group'), may hold values from 0 to 2, as said below
Outputs:
- dosage: float32 [2, 64], P(None, 'group')
- log_likelihood: float32 [2], replicated
Inputs may be any that keep to these rules, and one draw needn't show every extreme that they name: `genotypes`: 2 marks a marker at which the target's allele is missing; 0 and 1 are observed alleles.
All inputs are finite; a program needn't handle non-finite values. No bound on the sum of `panel_alleles` on one device may be relied on, other than what follows from the above.
Results may differ from a plain program's by a relative error of at most 0.0003.
Values sent between devices are 32-bit elements; how exact they have to be, the bound alone decides.
A program may use at most 64 MiB of HBM per device.

v0:
```python
import jax
import jax.numpy as jnp
from jax import lax
from jax.sharding import PartitionSpec as P

K = 131072
MISMATCH = 0.05
HIGHEST = lax.Precision.HIGHEST


def from_behind(x, axis, by):
    peers = lax.axis_size(axis)
    pairs = [(i, i + by) for i in range(peers) if 0 <= i + by < peers]
    return lax.ppermute(x, axis, pairs)


def emission(panel_rows, geno_col):
    observed = geno_col[:, None]
    agrees = jnp.where(panel_rows == observed, 1.0 - MISMATCH, MISMATCH)
    return jnp.where(observed == 2, 1.0, agrees).astype(jnp.float32)


def forward_terms(panel_rows, geno_col, switches):
    emitted = emission(panel_rows, geno_col)
    retain = emitted * (1.0 - switches)[:, None]
    inject = emitted * (switches / K)[:, None]
    return (retain, inject, None)


def backward_terms(panel_rows, geno_col, switches):
    emitted = emission(panel_rows, geno_col)[::-1]
    flipped = switches[::-1]
    retain = emitted * (1.0 - flipped)[:, None]
    inject = jnp.broadcast_to((flipped / K)[:, None], emitted.shape)
    return (retain, inject, emitted)


def partial_sums(entering, retain, inject, weight, extent):
    logs = jnp.cumsum(jnp.log(retain), axis=0)
    shifted = jnp.concatenate([jnp.zeros_like(entering)[None], logs[: extent - 1]], axis=0)
    before = jnp.exp(shifted)
    left_side = before if weight is None else weight * before
    leading = jnp.einsum("jk,k->j", left_side, entering, precision=HIGHEST)
    anchor = shifted[0]
    right_side = inject * jnp.exp(anchor[None] - logs)
    nearby = jnp.exp(jnp.minimum(shifted - anchor[None], 0.0))
    nearby = nearby if weight is None else weight * nearby
    columns = [jnp.einsum("jk,tk->jt", nearby, right_side, precision=HIGHEST)]
    coupling = jnp.concatenate(columns, axis=1)
    return (leading, coupling)


def solve_sums(leading, coupling):
    columns = coupling.shape[1]

    def settle(marker, sigmas):
        below = jnp.arange(columns) < marker
        update = leading[marker] + jnp.sum(
            jnp.where(below, coupling[marker] * sigmas[:columns], 0.0)
        )
        return sigmas.at[marker].set(update)

    return lax.fori_loop(0, leading.shape[0], settle, jnp.zeros_like(leading))


def advance(entering, retain, inject, sigmas, keep_states):

    def advance_single(current, pieces):
        current = pieces[0] * current + pieces[1] * pieces[2]
        return (current, current if keep_states else None)

    return lax.scan(advance_single, entering, (retain, inject, sigmas[: retain.shape[0]]))


def place_rows(store, block, active):
    return jnp.where(active, block, store)


def on_device(panel_alleles, recomb_rates, genotypes):
    chain_size = lax.axis_size("group")
    position = lax.axis_index("group")
    markers, width = panel_alleles.shape
    targets = genotypes.shape[0]
    bundles = targets // targets
    uniform = jnp.full((targets, width), 1.0 / K, jnp.float32)
    first_row = position == 0
    last_row = position == chain_size - 1

    def local_sums(active, arrivals, geno_rows, maker, extent):

        def local_compute():

            def local_single(pieces):
                retain, inject, weight = maker(panel_alleles, pieces[1], recomb_rates)
                return partial_sums(pieces[0], retain, inject, weight, extent)

            return lax.map(local_single, (arrivals, geno_rows))

        def local_skipped():
            return (
                jnp.zeros((targets, extent), jnp.float32),
                jnp.zeros((targets, extent, markers), jnp.float32),
            )

        return lax.cond(active, local_compute, local_skipped)

    def outgoing(active, arrivals, geno_rows, sigmas, maker, scale_row):

        def outgoing_compute():

            def outgoing_single(pieces):
                retain, inject, weight = maker(panel_alleles, pieces[1], recomb_rates)
                ending, unused = advance(pieces[0], retain, inject, pieces[2], False)
                return ending / pieces[2][scale_row]

            return lax.map(outgoing_single, (arrivals, geno_rows, sigmas))

        def outgoing_skipped():
            return jnp.zeros((targets, width), jnp.float32)

        return lax.cond(active, outgoing_compute, outgoing_skipped)

    def moment_step(moment, carried_state):
        (
            sent_forward,
            sent_backward,
            sent_running,
            store_forward,
            store_backward,
            sigma_forward,
            sigma_backward,
            log_terms,
        ) = carried_state
        got_forward = from_behind(sent_forward, "group", 1)
        got_backward = from_behind(sent_backward, "group", -1)
        entering_forward = jnp.where(first_row, uniform, got_forward)
        entering_backward = jnp.where(last_row, uniform, got_backward)
        index_forward = moment - position
        index_backward = moment - (chain_size - 1 - position)
        active_forward = (index_forward >= 0) & (index_forward < bundles)
        active_backward = (index_backward >= 0) & (index_backward < bundles)
        lead_forward, couple_forward = local_sums(
            active_forward, entering_forward, genotypes, forward_terms, markers + 1
        )
        lead_backward, couple_backward = local_sums(
            active_backward, entering_backward, genotypes, backward_terms, markers
        )
        lead_forward, couple_forward, lead_backward, couple_backward = lax.psum(
            (lead_forward, couple_forward, lead_backward, couple_backward), "batch"
        )
        sigmas_forward = jax.vmap(solve_sums)(lead_forward, couple_forward)
        sigmas_backward = jax.vmap(solve_sums)(lead_backward, couple_backward)
        next_forward = outgoing(
            active_forward, entering_forward, genotypes, sigmas_forward, forward_terms, markers
        )
        next_backward = outgoing(
            active_backward,
            entering_backward,
            genotypes,
            sigmas_backward,
            backward_terms,
            markers - 1,
        )
        guarded = jnp.where(active_forward, sigmas_forward[:, markers], 1.0)
        running = jnp.log(guarded)
        store_forward = place_rows(store_forward, entering_forward, active_forward)
        store_backward = place_rows(store_backward, entering_backward, active_backward)
        sigma_forward = place_rows(sigma_forward, sigmas_forward, active_forward)
        sigma_backward = place_rows(sigma_backward, sigmas_backward, active_backward)
        log_terms = place_rows(log_terms, running, active_forward)
        return (
            next_forward,
            next_backward,
            running,
            store_forward,
            store_backward,
            sigma_forward,
            sigma_backward,
            log_terms,
        )

    initial = (
        jnp.zeros((targets, width), jnp.float32),
        jnp.zeros((targets, width), jnp.float32),
        jnp.zeros((targets,), jnp.float32),
        jnp.zeros((targets, width), jnp.float32),
        jnp.zeros((targets, width), jnp.float32),
        jnp.zeros((targets, markers + 1), jnp.float32),
        jnp.zeros((targets, markers), jnp.float32),
        jnp.zeros((targets,), jnp.float32),
    )
    final_state = lax.fori_loop(0, chain_size + bundles - 1, moment_step, initial)
    store_forward, store_backward, sigma_forward, sigma_backward, log_terms = final_state[3:]
    whole_log = lax.psum(log_terms, "group")
    log_likelihood = whole_log / (markers * chain_size)

    def posterior(pieces):
        entering_ahead, entering_behind, geno_col, sigmas_ahead, sigmas_behind = pieces
        retain, inject, weight = forward_terms(panel_alleles, geno_col, recomb_rates)
        unused_f, forward_states = advance(entering_ahead, retain, inject, sigmas_ahead, True)
        forward_rows = forward_states / sigmas_ahead[1:, None]
        retain, inject, weight = backward_terms(panel_alleles, geno_col, recomb_rates)
        unused_b, backward_states = advance(entering_behind, retain, inject, sigmas_behind, True)
        scaled_back = backward_states[:-1] / sigmas_behind[:-1, None]
        backward_rows = jnp.concatenate([entering_behind[None], scaled_back], axis=0)[::-1]
        product = forward_rows * backward_rows
        numerator = jnp.sum(jnp.where(panel_alleles == 1, product, 0.0), axis=1)
        return (numerator, jnp.sum(product, axis=1))

    numerator, denominator = lax.map(
        posterior, (store_forward, store_backward, genotypes, sigma_forward, sigma_backward)
    )
    numerator, denominator = lax.psum((numerator, denominator), "batch")
    return (numerator / denominator, log_likelihood)


def solution(mesh):
    placed = (P("group", "batch"), P("group"), P(None, "group"))
    return jax.shard_map(
        on_device, mesh=mesh, in_specs=placed, out_specs=(P(None, "group"), P()), check_vma=False
    )
```

profile of v0, /device:TPU:1, one launch (start us, length us, event | category | flops | bytes accessed | tf_op | source)
XLA Modules:
  0.0 1798.0 jit_solution(14653522750120755591)
XLA Ops:
  2.0 1592.2 %while.198 = (s32[]{:T(128)}, f32[2,4096]{1,0:T(2,128)}, f32[2,4096]{1,0:T(2,128)}, f32[2,4096]{1,0:T(2,128)S(1)}, f32[2,4096]{1,0:T(2,128)S(1)}, /*index=5*/f32...) while((s32[]{:T(128)}, f32[2,4096]{1,0:T(2,128)}, ...), condition=%wide.region_35.36_spmd.clone, body=%wide.region_0.35_spmd.clone.sunk | while | flops 9048711 | bytes 5607151 | solution.py:192
  14.0 118.2 %all-reduce.5 = (f32[2,9]{1,0:T(2,128)S(1)}, f32[2,9,8]{2,0,1:T(2,128)S(1)}, f32[2,8]{1,0:T(2,128)S(1)}, f32[2,8,8]{2,0,1:T(2,128)S(1)}) all-reduce(f32[2,9]{1,0:T(2,128)} %get-tuple-element.1830, f32[2,9,8]{2,0,1:T(2,128)S(1)} %copy.29, f32[2,8]{1,0:T(2,128)} %get-tuple-element.1833, ...), channel_id=1, replica_groups=mesh['group'=8,'batch'=32] {'batch'}, use_global_device_ids=true, to_apply=%region_6.6 | all-reduce | flops 306 | bytes 2448 | tf_op jit(solution)/shard_map/while/body/eval_jaxpr/psum | solution.py:148
  132.2 17.9 while.201
  167.2 30.1 %collective-permute-start = (f32[2,4096]{1,0:T(2,128)}, f32[2,4096]{1,0:T(2,128)S(1)}, u32[]{:S(2)}, u32[]{:S(2)}) collective-permute-start(f32[2,4096]{1,0:T(2,128)} %get-tuple-element.2213), channel_id=1, source_target_pairs={{0,32},{32,64},{64,96},{96,128},{128,160},{160,192},{192,224},{1,3... | collective-permute-start | bytes 98312 | tf_op jit(solution)/shard_map/while/body/eval_jaxpr/ppermute | solution.py:14
  197.3 28.5 %collective-permute-start.1 = (f32[2,4096]{1,0:T(2,128)}, f32[2,4096]{1,0:T(2,128)S(1)}, u32[]{:S(2)}, u32[]{:S(2)}) collective-permute-start(f32[2,4096]{1,0:T(2,128)} %get-tuple-element.2214), channel_id=1, source_target_pairs={{32,0},{64,32},{96,64},{128,96},{160,128},{192,160},{224,192},{33,... | collective-permute-start | bytes 98312 | tf_op jit(solution)/shard_map/while/body/eval_jaxpr/ppermute | solution.py:14
  234.8 110.5 %all-reduce.5 = (f32[2,9]{1,0:T(2,128)S(1)}, f32[2,9,8]{2,0,1:T(2,128)S(1)}, f32[2,8]{1,0:T(2,128)S(1)}, f32[2,8,8]{2,0,1:T(2,128)S(1)}) all-reduce(f32[2,9]{1,0:T(2,128)} %get-tuple-element.1830, f32[2,9,8]{2,0,1:T(2,128)S(1)} %copy.29, f32[2,8]{1,0:T(2,128)} %get-tuple-element.1833, ...), channel_id=1, replica_groups=mesh['group'=8,'batch'=32] {'batch'}, use_global_device_ids=true, to_apply=%region_6.6 | all-reduce | flops 306 | bytes 2448 | tf_op jit(solution)/shard_map/while/body/eval_jaxpr/psum | solution.py:148
  345.3 17.9 while.201
  379.6 26.4 %conditional.14 = (f32[2,4096]{1,0:T(2,128)}) conditional(s32[]{:T(128)} %convert_element_type.22, () %tuple.344, (f32[2,4096]{1,0:T(2,128)S(1)}, s32[2,8]{1,0:T(2,128)S(1)}, s32[8,4096]{1,0:T(8,128)S(1)}, f32[8]{0:T(128)S(1)}, f32[2,9]{1,0:T(2,128)S(1)}) %tuple.427), branch_computations={%region_12.12_spmd, %region_13.17_spmd} | conditional | flops 245788 | bytes 688914 | solution.py:121
  379.6 26.4 %while.184 = (s32[]{:T(128)}, f32[2,4096]{1,0:T(2,128)}, f32[2,4096]{1,0:T(2,128)S(1)}, s32[2,8]{1,0:T(2,128)S(1)}, s32[8,4096]{1,0:T(8,128)S(1)}, /*index=5*/f3...) while((s32[]{:T(128)}, f32[2,4096]{1,0:T(2,128)}, f32[2,4096]{1,0:T(2,128)S(1)}, ...), condition=%wide.region_17.16_spmd, body=%wide.region_14.15_spmd.sunk | while | flops 245788 | bytes 688818 | solution.py:116
  415.5 110.3 %all-reduce.5 = (f32[2,9]{1,0:T(2,128)S(1)}, f32[2,9,8]{2,0,1:T(2,128)S(1)}, f32[2,8]{1,0:T(2,128)S(1)}, f32[2,8,8]{2,0,1:T(2,128)S(1)}) all-reduce(f32[2,9]{1,0:T(2,128)} %get-tuple-element.1830, f32[2,9,8]{2,0,1:T(2,128)S(1)} %copy.29, f32[2,8]{1,0:T(2,128)} %get-tuple-element.1833, ...), channel_id=1, replica_groups=mesh['group'=8,'batch'=32] {'batch'}, use_global_device_ids=true, to_apply=%region_6.6 | all-reduce | flops 306 | bytes 2448 | tf_op jit(solution)/shard_map/while/body/eval_jaxpr/psum | solution.py:148
  560.8 60.6 %collective-permute-start = (f32[2,4096]{1,0:T(2,128)}, f32[2,4096]{1,0:T(2,128)S(1)}, u32[]{:S(2)}, u32[]{:S(2)}) collective-permute-start(f32[2,4096]{1,0:T(2,128)} %get-tuple-element.2213), channel_id=1, source_target_pairs={{0,32},{32,64},{64,96},{96,128},{128,160},{160,192},{192,224},{1,3... | collective-permute-start | bytes 98312 | tf_op jit(solution)/shard_map/while/body/eval_jaxpr/ppermute | solution.py:14
  628.8 110.7 %all-reduce.5 = (f32[2,9]{1,0:T(2,128)S(1)}, f32[2,9,8]{2,0,1:T(2,128)S(1)}, f32[2,8]{1,0:T(2,128)S(1)}, f32[2,8,8]{2,0,1:T(2,128)S(1)}) all-reduce(f32[2,9]{1,0:T(2,128)} %get-tuple-element.1830, f32[2,9,8]{2,0,1:T(2,128)S(1)} %copy.29, f32[2,8]{1,0:T(2,128)} %get-tuple-element.1833, ...), channel_id=1, replica_groups=mesh['group'=8,'batch'=32] {'batch'}, use_global_device_ids=true, to_apply=%region_6.6 | all-reduce | flops 306 | bytes 2448 | tf_op jit(solution)/shard_map/while/body/eval_jaxpr/psum | solution.py:148
  774.5 29.3 %collective-permute-start = (f32[2,4096]{1,0:T(2,128)}, f32[2,4096]{1,0:T(2,128)S(1)}, u32[]{:S(2)}, u32[]{:S(2)}) collective-permute-start(f32[2,4096]{1,0:T(2,128)} %get-tuple-element.2213), channel_id=1, source_target_pairs={{0,32},{32,64},{64,96},{96,128},{128,160},{160,192},{192,224},{1,3... | collective-permute-start | bytes 98312 | tf_op jit(solution)/shard_map/while/body/eval_jaxpr/ppermute | solution.py:14
  811.7 110.1 %all-reduce.5 = (f32[2,9]{1,0:T(2,128)S(1)}, f32[2,9,8]{2,0,1:T(2,128)S(1)}, f32[2,8]{1,0:T(2,128)S(1)}, f32[2,8,8]{2,0,1:T(2,128)S(1)}) all-reduce(f32[2,9]{1,0:T(2,128)} %get-tuple-element.1830, f32[2,9,8]{2,0,1:T(2,128)S(1)} %copy.29, f32[2,8]{1,0:T(2,128)} %get-tuple-element.1833, ...), channel_id=1, replica_groups=mesh['group'=8,'batch'=32] {'batch'}, use_global_device_ids=true, to_apply=%region_6.6 | all-reduce | flops 306 | bytes 2448 | tf_op jit(solution)/shard_map/while/body/eval_jaxpr/psum | solution.py:148
  956.8 47.8 %collective-permute-start = (f32[2,4096]{1,0:T(2,128)}, f32[2,4096]{1,0:T(2,128)S(1)}, u32[]{:S(2)}, u32[]{:S(2)}) collective-permute-start(f32[2,4096]{1,0:T(2,128)} %get-tuple-element.2213), channel_id=1, source_target_pairs={{0,32},{32,64},{64,96},{96,128},{128,160},{160,192},{192,224},{1,3... | collective-permute-start | bytes 98312 | tf_op jit(solution)/shard_map/while/body/eval_jaxpr/ppermute | solution.py:14
  1020.1 110.2 %all-reduce.5 = (f32[2,9]{1,0:T(2,128)S(1)}, f32[2,9,8]{2,0,1:T(2,128)S(1)}, f32[2,8]{1,0:T(2,128)S(1)}, f32[2,8,8]{2,0,1:T(2,128)S(1)}) all-reduce(f32[2,9]{1,0:T(2,128)} %get-tuple-element.1830, f32[2,9,8]{2,0,1:T(2,128)S(1)} %copy.29, f32[2,8]{1,0:T(2,128)} %get-tuple-element.1833, ...), channel_id=1, replica_groups=mesh['group'=8,'batch'=32] {'batch'}, use_global_device_ids=true, to_apply=%region_6.6 | all-reduce | flops 306 | bytes 2448 | tf_op jit(solution)/shard_map/while/body/eval_jaxpr/psum | solution.py:148
  1165.3 86.8 %collective-permute-start = (f32[2,4096]{1,0:T(2,128)}, f32[2,4096]{1,0:T(2,128)S(1)}, u32[]{:S(2)}, u32[]{:S(2)}) collective-permute-start(f32[2,4096]{1,0:T(2,128)} %get-tuple-element.2213), channel_id=1, source_target_pairs={{0,32},{32,64},{64,96},{96,128},{128,160},{160,192},{192,224},{1,3... | collective-permute-start | bytes 98312 | tf_op jit(solution)/shard_map/while/body/eval_jaxpr/ppermute | solution.py:14
  1265.7 110.3 %all-reduce.5 = (f32[2,9]{1,0:T(2,128)S(1)}, f32[2,9,8]{2,0,1:T(2,128)S(1)}, f32[2,8]{1,0:T(2,128)S(1)}, f32[2,8,8]{2,0,1:T(2,128)S(1)}) all-reduce(f32[2,9]{1,0:T(2,128)} %get-tuple-element.1830, f32[2,9,8]{2,0,1:T(2,128)S(1)} %copy.29, f32[2,8]{1,0:T(2,128)} %get-tuple-element.1833, ...), channel_id=1, replica_groups=mesh['group'=8,'batch'=32] {'batch'}, use_global_device_ids=true, to_apply=%region_6.6 | all-reduce | flops 306 | bytes 2448 | tf_op jit(solution)/shard_map/while/body/eval_jaxpr/psum | solution.py:148
  1409.8 28.6 %conditional.15 = (f32[2,4096]{1,0:T(2,128)}) conditional(s32[]{:T(128)} %convert_element_type.23, () %tuple.351, (f32[2,4096]{1,0:T(2,128)S(1)}, s32[2,8]{1,0:T(2,128)S(1)}, s32[8,4096]{1,0:T(8,128)S(1)}, f32[8]{0:T(128)S(1)}, f32[2,8]{1,0:T(2,128)S(1)}) %tuple.426), branch_computations={%region_29.29_spmd, %region_30.34_spmd} | conditional | flops 147484 | bytes 1147718 | solution.py:121
  1409.8 28.6 %while.188 = (s32[]{:T(128)}, f32[2,4096]{1,0:T(2,128)}, f32[2,4096]{1,0:T(2,128)S(1)}, s32[2,8]{1,0:T(2,128)S(1)}, s32[8,4096]{1,0:T(8,128)S(1)}, /*index=5*/f3...) while((s32[]{:T(128)}, f32[2,4096]{1,0:T(2,128)}, f32[2,4096]{1,0:T(2,128)S(1)}, ...), condition=%wide.region_34.33_spmd, body=%wide.region_31.32_spmd.sunk | while | flops 147484 | bytes 1147622 | solution.py:116
  1448.5 110.6 %all-reduce.5 = (f32[2,9]{1,0:T(2,128)S(1)}, f32[2,9,8]{2,0,1:T(2,128)S(1)}, f32[2,8]{1,0:T(2,128)S(1)}, f32[2,8,8]{2,0,1:T(2,128)S(1)}) all-reduce(f32[2,9]{1,0:T(2,128)} %get-tuple-element.1830, f32[2,9,8]{2,0,1:T(2,128)S(1)} %copy.29, f32[2,8]{1,0:T(2,128)} %get-tuple-element.1833, ...), channel_id=1, replica_groups=mesh['group'=8,'batch'=32] {'batch'}, use_global_device_ids=true, to_apply=%region_6.6 | all-reduce | flops 306 | bytes 2448 | tf_op jit(solution)/shard_map/while/body/eval_jaxpr/psum | solution.py:148
  1594.1 61.6 %while.195 = (s32[]{:T(128)}, f32[2,8]{1,0:T(2,128)S(1)}, f32[2,8]{1,0:T(2,128)S(1)}, s32[8,4096]{1,0:T(8,128)}, f32[2,4096]{1,0:T(2,128)S(1)}, /*index=5*/s32[2...) while((s32[]{:T(128)}, f32[2,8]{1,0:T(2,128)S(1)}, ...), condition=%wide.region_43.44_spmd, body=%wide.region_36.43_spmd.sunk | while | flops 479262 | bytes 3671731 | solution.py:210
  1655.7 55.7 %all-reduce.3 = (f32[2,8]{1,0:T(2,128)S(1)}, f32[2,8]{1,0:T(2,128)S(1)}) all-reduce(f32[2,8]{1,0:T(2,128)S(1)} %get-tuple-element.921, f32[2,8]{1,0:T(2,128)S(1)} %get-tuple-element.922), channel_id=1, replica_groups=mesh['group'=8,'batch'=32] {'batch'}, use_global_device_ids=true, to_apply=%region_44.45 | all-reduce | flops 32 | bytes 256 | tf_op jit(solution)/shard_map/psum | solution.py:213
  1712.0 85.4 %psum.71 = f32[2]{0:T(128)S(1)} all-reduce(f32[2]{0:T(128)S(1)} %get-tuple-element.923), channel_id=1, replica_groups=mesh['group'=8,'batch'=32] {'group'}, use_global_device_ids=true, to_apply=%region_46.47 | all-reduce | flops 2 | bytes 16 | tf_op jit(solution)/shard_map/psum | solution.py:194
  (1819 shorter events, 858.4 us)
Async XLA Ops:
  2.0 6.6 copy-start
  2.0 6.6 collective-permute-start
  6.6 5.4 collective-permute-start.1
  167.2 58.7 %copy-start = (s32[8,4096]{1,0:T(8,128)S(1)}, s32[8,4096]{1,0:T(8,128)}, u32[]{:S(2)}) copy-start(s32[8,4096]{1,0:T(8,128)} %get-tuple-element.2247) | copy-start | bytes 393220 | tf_op jit(solution)/shard_map/while
  167.2 58.6 %collective-permute-start = (f32[2,4096]{1,0:T(2,128)}, f32[2,4096]{1,0:T(2,128)S(1)}, u32[]{:S(2)}, u32[]{:S(2)}) collective-permute-start(f32[2,4096]{1,0:T(2,128)} %get-tuple-element.2213), channel_id=1, source_target_pairs={{0,32},{32,64},{64,96},{96,128},{128,160},{160,192},{192,224},{1,3... | collective-permute-start | bytes 98312 | tf_op jit(solution)/shard_map/while/body/eval_jaxpr/ppermute | solution.py:14
  197.3 35.5 %collective-permute-start.1 = (f32[2,4096]{1,0:T(2,128)}, f32[2,4096]{1,0:T(2,128)S(1)}, u32[]{:S(2)}, u32[]{:S(2)}) collective-permute-start(f32[2,4096]{1,0:T(2,128)} %get-tuple-element.2214), channel_id=1, source_target_pairs={{32,0},{64,32},{96,64},{128,96},{160,128},{192,160},{224,192},{33,... | collective-permute-start | bytes 98312 | tf_op jit(solution)/shard_map/while/body/eval_jaxpr/ppermute | solution.py:14
  406.1 4.5 collective-permute-start
  408.1 5.4 collective-permute-start.1
  560.8 62.6 %copy-start = (s32[8,4096]{1,0:T(8,128)S(1)}, s32[8,4096]{1,0:T(8,128)}, u32[]{:S(2)}) copy-start(s32[8,4096]{1,0:T(8,128)} %get-tuple-element.2247) | copy-start | bytes 393220 | tf_op jit(solution)/shard_map/while
  560.8 62.5 %collective-permute-start = (f32[2,4096]{1,0:T(2,128)}, f32[2,4096]{1,0:T(2,128)S(1)}, u32[]{:S(2)}, u32[]{:S(2)}) collective-permute-start(f32[2,4096]{1,0:T(2,128)} %get-tuple-element.2213), channel_id=1, source_target_pairs={{0,32},{32,64},{64,96},{96,128},{128,160},{160,192},{192,224},{1,3... | collective-permute-start | bytes 98312 | tf_op jit(solution)/shard_map/while/body/eval_jaxpr/ppermute | solution.py:14
  621.4 5.4 collective-permute-start.1
  774.5 31.4 %copy-start = (s32[8,4096]{1,0:T(8,128)S(1)}, s32[8,4096]{1,0:T(8,128)}, u32[]{:S(2)}) copy-start(s32[8,4096]{1,0:T(8,128)} %get-tuple-element.2247) | copy-start | bytes 393220 | tf_op jit(solution)/shard_map/while
  774.5 31.3 %collective-permute-start = (f32[2,4096]{1,0:T(2,128)}, f32[2,4096]{1,0:T(2,128)S(1)}, u32[]{:S(2)}, u32[]{:S(2)}) collective-permute-start(f32[2,4096]{1,0:T(2,128)} %get-tuple-element.2213), channel_id=1, source_target_pairs={{0,32},{32,64},{64,96},{96,128},{128,160},{160,192},{192,224},{1,3... | collective-permute-start | bytes 98312 | tf_op jit(solution)/shard_map/while/body/eval_jaxpr/ppermute | solution.py:14
  803.8 6.0 collective-permute-start.1
  956.8 49.8 %copy-start = (s32[8,4096]{1,0:T(8,128)S(1)}, s32[8,4096]{1,0:T(8,128)}, u32[]{:S(2)}) copy-start(s32[8,4096]{1,0:T(8,128)} %get-tuple-element.2247) | copy-start | bytes 393220 | tf_op jit(solution)/shard_map/while
  956.8 49.7 %collective-permute-start = (f32[2,4096]{1,0:T(2,128)}, f32[2,4096]{1,0:T(2,128)S(1)}, u32[]{:S(2)}, u32[]{:S(2)}) collective-permute-start(f32[2,4096]{1,0:T(2,128)} %get-tuple-element.2213), channel_id=1, source_target_pairs={{0,32},{32,64},{64,96},{96,128},{128,160},{160,192},{192,224},{1,3... | collective-permute-start | bytes 98312 | tf_op jit(solution)/shard_map/while/body/eval_jaxpr/ppermute | solution.py:14
  1004.6 13.5 collective-permute-start.1
  1165.3 88.8 %copy-start = (s32[8,4096]{1,0:T(8,128)S(1)}, s32[8,4096]{1,0:T(8,128)}, u32[]{:S(2)}) copy-start(s32[8,4096]{1,0:T(8,128)} %get-tuple-element.2247) | copy-start | bytes 393220 | tf_op jit(solution)/shard_map/while
  1165.3 88.8 %collective-permute-start = (f32[2,4096]{1,0:T(2,128)}, f32[2,4096]{1,0:T(2,128)S(1)}, u32[]{:S(2)}, u32[]{:S(2)}) collective-permute-start(f32[2,4096]{1,0:T(2,128)} %get-tuple-element.2213), channel_id=1, source_target_pairs={{0,32},{32,64},{64,96},{96,128},{128,160},{160,192},{192,224},{1,3... | collective-permute-start | bytes 98312 | tf_op jit(solution)/shard_map/while/body/eval_jaxpr/ppermute | solution.py:14
  1252.1 5.4 collective-permute-start.1
  1439.1 4.5 collective-permute-start
  1441.1 5.4 collective-permute-start.1
  1610.8 13.9 copy-start.1
  1641.6 13.9 copy-start.1
  (4 other events, 10.5 us)
where the time goes:
time: 1800 us
  blocking collectives  1030 us (57%)
  starting transfers between devices  306 us (17%)
  other arithmetic  271 us (15%)
  local copies, waits for them, and re-layouts  159 us (9%)
  waiting for transfers between devices  18 us (1%)
    psum x8, blocking collectives, moment_step(): lax.psum((lead_forward, couple_forward, lead_backward, couple_backward),...  891 us
    ppermute x16, starting transfers between devices, from_behind(): return lax.ppermute(x, axis, pairs)  306 us
    another operation x280, other arithmetic  185 us
    psum x1, blocking collectives, on_device(): whole_log = lax.psum(log_terms, 'group')  85.4 us
    another operation x472, local copies, waits for them, and re-layouts  62.7 us
    psum x1, blocking collectives, on_device(): numerator, denominator = lax.psum((numerator, denominator), 'batch')  55.7 us
    mul x64, other arithmetic, advance_single(): current = pieces[0] * current + pieces[1] * pieces[2]  41.4 us
    dynamic_slice x64, local copies, waits for them, and re-layouts, advance(): lax.scan(advance_single, entering, (retain, inject, sigmas[:retain.shape[...  40.6 us
  transfers between devices with their start and end apart: 16, of which 7 were waited for; matrix products, arithmetic and copies ran while one was open for 1% of the time, Pallas kernels for 0%

commit v1 on v0

--- a/solution.py
+++ b/solution.py
@@ -191,7 +191,7 @@
     )
     final_state = lax.fori_loop(0, chain_size + bundles - 1, moment_step, initial)
     store_forward, store_backward, sigma_forward, sigma_backward, log_terms = final_state[3:]
-    whole_log = lax.psum(log_terms, "group")
+    whole_log = jnp.sum(lax.all_gather(log_terms, "group"), axis=0)
     log_likelihood = whole_log / (markers * chain_size)
 
     def posterior(pieces):

time: 1800 us -> 1780 us (0.989)
    psum x1 -> x0, blocking collectives: 85.4 us -> none  [on_device(): whole_log = lax.psum(log_terms, 'group')]
    unnamed x0 -> x1, blocking collectives: none -> 83.3 us
where the time goes in v1:
time: 1780 us
  blocking collectives  1030 us (58%)
  starting transfers between devices  296 us (17%)
  other arithmetic  268 us (15%)
  local copies, waits for them, and re-layouts  158 us (9%)
    psum x8, blocking collectives, moment_step(): lax.psum((lead_forward, couple_forward, lead_backward, couple_backward),...  891 us
    ppermute x16, starting transfers between devices, from_behind(): return lax.ppermute(x, axis, pairs)  296 us
    another operation x280, other arithmetic  185 us
    unnamed x1, blocking collectives  83.3 us
    another operation x472, local copies, waits for them, and re-layouts  62.5 us
    psum x1, blocking collectives, on_device(): numerator, denominator = lax.psum((numerator, denominator), 'batch')  55.7 us
    mul x64, other arithmetic, advance_single(): current = pieces[0] * current + pieces[1] * pieces[2]  38.6 us
    dynamic_slice x64, local copies, waits for them, and re-layouts, advance(): lax.scan(advance_single, entering, (retain, inject, sigmas[:retain.shape[...  38.2 us
  transfers between devices with their start and end apart: 16, of which 7 were waited for; matrix products, arithmetic and copies ran while one was open for 1% of the time, Pallas kernels for 0%

profile of v1, /device:TPU:1, one launch (start us, length us, event | category | flops | bytes accessed | tf_op | source)
XLA Modules:
  0.0 1780.7 jit_solution(11381091232334486923)
XLA Ops:
  2.0 1578.5 %while.198 = (s32[]{:T(128)}, f32[2,4096]{1,0:T(2,128)}, f32[2,4096]{1,0:T(2,128)}, f32[2,4096]{1,0:T(2,128)S(1)}, f32[2,4096]{1,0:T(2,128)S(1)}, /*index=5*/f32...) while((s32[]{:T(128)}, f32[2,4096]{1,0:T(2,128)}, ...), condition=%wide.region_35.36_spmd.clone, body=%wide.region_0.35_spmd.clone.sunk | while | flops 9048711 | bytes 5607151 | solution.py:192
  14.0 118.2 %all-reduce.6 = (f32[2,9]{1,0:T(2,128)S(1)}, f32[2,9,8]{2,0,1:T(2,128)S(1)}, f32[2,8]{1,0:T(2,128)S(1)}, f32[2,8,8]{2,0,1:T(2,128)S(1)}) all-reduce(f32[2,9]{1,0:T(2,128)} %get-tuple-element.1830, f32[2,9,8]{2,0,1:T(2,128)S(1)} %copy.29, f32[2,8]{1,0:T(2,128)} %get-tuple-element.1833, ...), channel_id=1, replica_groups=mesh['group'=8,'batch'=32] {'batch'}, use_global_device_ids=true, to_apply=%region_6.6 | all-reduce | flops 306 | bytes 2448 | tf_op jit(solution)/shard_map/while/body/eval_jaxpr/psum | solution.py:148
  167.2 30.1 %collective-permute-start = (f32[2,4096]{1,0:T(2,128)}, f32[2,4096]{1,0:T(2,128)S(1)}, u32[]{:S(2)}, u32[]{:S(2)}) collective-permute-start(f32[2,4096]{1,0:T(2,128)} %get-tuple-element.2213), channel_id=1, source_target_pairs={{0,32},{32,64},{64,96},{96,128},{128,160},{160,192},{192,224},{1,3... | collective-permute-start | bytes 98312 | tf_op jit(solution)/shard_map/while/body/eval_jaxpr/ppermute | solution.py:14
  197.3 29.0 %collective-permute-start.1 = (f32[2,4096]{1,0:T(2,128)}, f32[2,4096]{1,0:T(2,128)S(1)}, u32[]{:S(2)}, u32[]{:S(2)}) collective-permute-start(f32[2,4096]{1,0:T(2,128)} %get-tuple-element.2214), channel_id=1, source_target_pairs={{32,0},{64,32},{96,64},{128,96},{160,128},{192,160},{224,192},{33,... | collective-permute-start | bytes 98312 | tf_op jit(solution)/shard_map/while/body/eval_jaxpr/ppermute | solution.py:14
  235.2 110.5 %all-reduce.6 = (f32[2,9]{1,0:T(2,128)S(1)}, f32[2,9,8]{2,0,1:T(2,128)S(1)}, f32[2,8]{1,0:T(2,128)S(1)}, f32[2,8,8]{2,0,1:T(2,128)S(1)}) all-reduce(f32[2,9]{1,0:T(2,128)} %get-tuple-element.1830, f32[2,9,8]{2,0,1:T(2,128)S(1)} %copy.29, f32[2,8]{1,0:T(2,128)} %get-tuple-element.1833, ...), channel_id=1, replica_groups=mesh['group'=8,'batch'=32] {'batch'}, use_global_device_ids=true, to_apply=%region_6.6 | all-reduce | flops 306 | bytes 2448 | tf_op jit(solution)/shard_map/while/body/eval_jaxpr/psum | solution.py:148
  345.7 17.9 %while.201 = (s32[]{:T(128)}, f32[2,9]{1,0:T(2,128)S(1)}, f32[2,9]{1,0:T(2,128)S(1)}, f32[2,9,8]{2,0,1:T(2,128)S(1)}, s32[]{:T(128)}, /*index=5*/s32[1]{0:T(128)}, s32[]{:T(128)}) while((s32[]{:T(128)}, f32[2,9]{1,0:T(2,128)S(1)}, f32[2,9]{1,0:T(2,128)S(1)}, f32[2,9,8]{2,0,1:T(2,128)S(1)}, s32[]{:T(128)}, /*index=5*/s32[1]{0:T(128)}, ...), condition=%wide.region_11.11_spmd, body=%wide.region_8.10_spmd.sunk | while | flops 73 | bytes 623 | solution.py:63
  380.1 26.9 %conditional.14 = (f32[2,4096]{1,0:T(2,128)}) conditional(s32[]{:T(128)} %convert_element_type.22, () %tuple.344, (f32[2,4096]{1,0:T(2,128)S(1)}, s32[2,8]{1,0:T(2,128)S(1)}, s32[8,4096]{1,0:T(8,128)S(1)}, f32[8]{0:T(128)S(1)}, f32[2,9]{1,0:T(2,128)S(1)}) %tuple.427), branch_computations={%region_12.12_spmd, %region_13.17_spmd} | conditional | flops 245788 | bytes 688914 | solution.py:121
  380.1 26.9 %while.184 = (s32[]{:T(128)}, f32[2,4096]{1,0:T(2,128)}, f32[2,4096]{1,0:T(2,128)S(1)}, s32[2,8]{1,0:T(2,128)S(1)}, s32[8,4096]{1,0:T(8,128)S(1)}, /*index=5*/f3...) while((s32[]{:T(128)}, f32[2,4096]{1,0:T(2,128)}, f32[2,4096]{1,0:T(2,128)S(1)}, ...), condition=%wide.region_17.16_spmd, body=%wide.region_14.15_spmd.sunk | while | flops 245788 | bytes 688818 | solution.py:116
  416.5 110.3 %all-reduce.6 = (f32[2,9]{1,0:T(2,128)S(1)}, f32[2,9,8]{2,0,1:T(2,128)S(1)}, f32[2,8]{1,0:T(2,128)S(1)}, f32[2,8,8]{2,0,1:T(2,128)S(1)}) all-reduce(f32[2,9]{1,0:T(2,128)} %get-tuple-element.1830, f32[2,9,8]{2,0,1:T(2,128)S(1)} %copy.29, f32[2,8]{1,0:T(2,128)} %get-tuple-element.1833, ...), channel_id=1, replica_groups=mesh['group'=8,'batch'=32] {'batch'}, use_global_device_ids=true, to_apply=%region_6.6 | all-reduce | flops 306 | bytes 2448 | tf_op jit(solution)/shard_map/while/body/eval_jaxpr/psum | solution.py:148
  526.8 17.9 %while.201 = (s32[]{:T(128)}, f32[2,9]{1,0:T(2,128)S(1)}, f32[2,9]{1,0:T(2,128)S(1)}, f32[2,9,8]{2,0,1:T(2,128)S(1)}, s32[]{:T(128)}, /*index=5*/s32[1]{0:T(128)}, s32[]{:T(128)}) while((s32[]{:T(128)}, f32[2,9]{1,0:T(2,128)S(1)}, f32[2,9]{1,0:T(2,128)S(1)}, f32[2,9,8]{2,0,1:T(2,128)S(1)}, s32[]{:T(128)}, /*index=5*/s32[1]{0:T(128)}, ...), condition=%wide.region_11.11_spmd, body=%wide.region_8.10_spmd.sunk | while | flops 73 | bytes 623 | solution.py:63
  561.8 61.1 %collective-permute-start = (f32[2,4096]{1,0:T(2,128)}, f32[2,4096]{1,0:T(2,128)S(1)}, u32[]{:S(2)}, u32[]{:S(2)}) collective-permute-start(f32[2,4096]{1,0:T(2,128)} %get-tuple-element.2213), channel_id=1, source_target_pairs={{0,32},{32,64},{64,96},{96,128},{128,160},{160,192},{192,224},{1,3... | collective-permute-start | bytes 98312 | tf_op jit(solution)/shard_map/while/body/eval_jaxpr/ppermute | solution.py:14
  630.2 110.7 %all-reduce.6 = (f32[2,9]{1,0:T(2,128)S(1)}, f32[2,9,8]{2,0,1:T(2,128)S(1)}, f32[2,8]{1,0:T(2,128)S(1)}, f32[2,8,8]{2,0,1:T(2,128)S(1)}) all-reduce(f32[2,9]{1,0:T(2,128)} %get-tuple-element.1830, f32[2,9,8]{2,0,1:T(2,128)S(1)} %copy.29, f32[2,8]{1,0:T(2,128)} %get-tuple-element.1833, ...), channel_id=1, replica_groups=mesh['group'=8,'batch'=32] {'batch'}, use_global_device_ids=true, to_apply=%region_6.6 | all-reduce | flops 306 | bytes 2448 | tf_op jit(solution)/shard_map/while/body/eval_jaxpr/psum | solution.py:148
  775.9 29.4 %collective-permute-start = (f32[2,4096]{1,0:T(2,128)}, f32[2,4096]{1,0:T(2,128)S(1)}, u32[]{:S(2)}, u32[]{:S(2)}) collective-permute-start(f32[2,4096]{1,0:T(2,128)} %get-tuple-element.2213), channel_id=1, source_target_pairs={{0,32},{32,64},{64,96},{96,128},{128,160},{160,192},{192,224},{1,3... | collective-permute-start | bytes 98312 | tf_op jit(solution)/shard_map/while/body/eval_jaxpr/ppermute | solution.py:14
  813.6 110.5 %all-reduce.6 = (f32[2,9]{1,0:T(2,128)S(1)}, f32[2,9,8]{2,0,1:T(2,128)S(1)}, f32[2,8]{1,0:T(2,128)S(1)}, f32[2,8,8]{2,0,1:T(2,128)S(1)}) all-reduce(f32[2,9]{1,0:T(2,128)} %get-tuple-element.1830, f32[2,9,8]{2,0,1:T(2,128)S(1)} %copy.29, f32[2,8]{1,0:T(2,128)} %get-tuple-element.1833, ...), channel_id=1, replica_groups=mesh['group'=8,'batch'=32] {'batch'}, use_global_device_ids=true, to_apply=%region_6.6 | all-reduce | flops 306 | bytes 2448 | tf_op jit(solution)/shard_map/while/body/eval_jaxpr/psum | solution.py:148
  959.1 35.8 %collective-permute-start = (f32[2,4096]{1,0:T(2,128)}, f32[2,4096]{1,0:T(2,128)S(1)}, u32[]{:S(2)}, u32[]{:S(2)}) collective-permute-start(f32[2,4096]{1,0:T(2,128)} %get-tuple-element.2213), channel_id=1, source_target_pairs={{0,32},{32,64},{64,96},{96,128},{128,160},{160,192},{192,224},{1,3... | collective-permute-start | bytes 98312 | tf_op jit(solution)/shard_map/while/body/eval_jaxpr/ppermute | solution.py:14
  1007.9 110.0 %all-reduce.6 = (f32[2,9]{1,0:T(2,128)S(1)}, f32[2,9,8]{2,0,1:T(2,128)S(1)}, f32[2,8]{1,0:T(2,128)S(1)}, f32[2,8,8]{2,0,1:T(2,128)S(1)}) all-reduce(f32[2,9]{1,0:T(2,128)} %get-tuple-element.1830, f32[2,9,8]{2,0,1:T(2,128)S(1)} %copy.29, f32[2,8]{1,0:T(2,128)} %get-tuple-element.1833, ...), channel_id=1, replica_groups=mesh['group'=8,'batch'=32] {'batch'}, use_global_device_ids=true, to_apply=%region_6.6 | all-reduce | flops 306 | bytes 2448 | tf_op jit(solution)/shard_map/while/body/eval_jaxpr/psum | solution.py:148
  1152.9 87.7 %collective-permute-start = (f32[2,4096]{1,0:T(2,128)}, f32[2,4096]{1,0:T(2,128)S(1)}, u32[]{:S(2)}, u32[]{:S(2)}) collective-permute-start(f32[2,4096]{1,0:T(2,128)} %get-tuple-element.2213), channel_id=1, source_target_pairs={{0,32},{32,64},{64,96},{96,128},{128,160},{160,192},{192,224},{1,3... | collective-permute-start | bytes 98312 | tf_op jit(solution)/shard_map/while/body/eval_jaxpr/ppermute | solution.py:14
  1254.2 110.5 %all-reduce.6 = (f32[2,9]{1,0:T(2,128)S(1)}, f32[2,9,8]{2,0,1:T(2,128)S(1)}, f32[2,8]{1,0:T(2,128)S(1)}, f32[2,8,8]{2,0,1:T(2,128)S(1)}) all-reduce(f32[2,9]{1,0:T(2,128)} %get-tuple-element.1830, f32[2,9,8]{2,0,1:T(2,128)S(1)} %copy.29, f32[2,8]{1,0:T(2,128)} %get-tuple-element.1833, ...), channel_id=1, replica_groups=mesh['group'=8,'batch'=32] {'batch'}, use_global_device_ids=true, to_apply=%region_6.6 | all-reduce | flops 306 | bytes 2448 | tf_op jit(solution)/shard_map/while/body/eval_jaxpr/psum | solution.py:148
  1398.4 26.5 %conditional.15 = (f32[2,4096]{1,0:T(2,128)}) conditional(s32[]{:T(128)} %convert_element_type.23, () %tuple.351, (f32[2,4096]{1,0:T(2,128)S(1)}, s32[2,8]{1,0:T(2,128)S(1)}, s32[8,4096]{1,0:T(8,128)S(1)}, f32[8]{0:T(128)S(1)}, f32[2,8]{1,0:T(2,128)S(1)}) %tuple.426), branch_computations={%region_29.29_spmd, %region_30.34_spmd} | conditional | flops 147484 | bytes 1147718 | solution.py:121
  1398.4 26.5 %while.188 = (s32[]{:T(128)}, f32[2,4096]{1,0:T(2,128)}, f32[2,4096]{1,0:T(2,128)S(1)}, s32[2,8]{1,0:T(2,128)S(1)}, s32[8,4096]{1,0:T(8,128)S(1)}, /*index=5*/f3...) while((s32[]{:T(128)}, f32[2,4096]{1,0:T(2,128)}, f32[2,4096]{1,0:T(2,128)S(1)}, ...), condition=%wide.region_34.33_spmd, body=%wide.region_31.32_spmd.sunk | while | flops 147484 | bytes 1147622 | solution.py:116
  1434.9 110.5 %all-reduce.6 = (f32[2,9]{1,0:T(2,128)S(1)}, f32[2,9,8]{2,0,1:T(2,128)S(1)}, f32[2,8]{1,0:T(2,128)S(1)}, f32[2,8,8]{2,0,1:T(2,128)S(1)}) all-reduce(f32[2,9]{1,0:T(2,128)} %get-tuple-element.1830, f32[2,9,8]{2,0,1:T(2,128)S(1)} %copy.29, f32[2,8]{1,0:T(2,128)} %get-tuple-element.1833, ...), channel_id=1, replica_groups=mesh['group'=8,'batch'=32] {'batch'}, use_global_device_ids=true, to_apply=%region_6.6 | all-reduce | flops 306 | bytes 2448 | tf_op jit(solution)/shard_map/while/body/eval_jaxpr/psum | solution.py:148
  1580.5 57.8 %while.195 = (s32[]{:T(128)}, f32[2,8]{1,0:T(2,128)S(1)}, f32[2,8]{1,0:T(2,128)S(1)}, s32[8,4096]{1,0:T(8,128)}, f32[2,4096]{1,0:T(2,128)S(1)}, /*index=5*/s32[2...) while((s32[]{:T(128)}, f32[2,8]{1,0:T(2,128)S(1)}, ...), condition=%wide.region_43.44_spmd, body=%wide.region_36.43_spmd.sunk | while | flops 479262 | bytes 3671731 | solution.py:210
  1638.3 55.7 %all-reduce.4 = (f32[2,8]{1,0:T(2,128)S(1)}, f32[2,8]{1,0:T(2,128)S(1)}) all-reduce(f32[2,8]{1,0:T(2,128)S(1)} %get-tuple-element.921, f32[2,8]{1,0:T(2,128)S(1)} %get-tuple-element.922), channel_id=1, replica_groups=mesh['group'=8,'batch'=32] {'batch'}, use_global_device_ids=true, to_apply=%region_44.45 | all-reduce | flops 32 | bytes 256 | tf_op jit(solution)/shard_map/psum | solution.py:213
  1696.8 83.3 %all-reduce.2 = f32[16]{0:T(128)S(1)} all-reduce(f32[16]{0:T(128)S(1)} %dynamic-update-slice.18), channel_id=2, replica_groups=mesh['group'=8,'batch'=32] {'group'}, use_global_device_ids=true, to_apply=%add.2 | all-reduce | flops 16 | bytes 128
  (1826 shorter events, 846.8 us)
Async XLA Ops:
  2.0 6.6 copy-start
  2.0 6.6 collective-permute-start
  6.6 5.4 collective-permute-start.1
  167.2 59.2 %copy-start = (s32[8,4096]{1,0:T(8,128)S(1)}, s32[8,4096]{1,0:T(8,128)}, u32[]{:S(2)}) copy-start(s32[8,4096]{1,0:T(8,128)} %get-tuple-element.2247) | copy-start | bytes 393220 | tf_op jit(solution)/shard_map/while
  167.2 59.1 %collective-permute-start = (f32[2,4096]{1,0:T(2,128)}, f32[2,4096]{1,0:T(2,128)S(1)}, u32[]{:S(2)}, u32[]{:S(2)}) collective-permute-start(f32[2,4096]{1,0:T(2,128)} %get-tuple-element.2213), channel_id=1, source_target_pairs={{0,32},{32,64},{64,96},{96,128},{128,160},{160,192},{192,224},{1,3... | collective-permute-start | bytes 98312 | tf_op jit(solution)/shard_map/while/body/eval_jaxpr/ppermute | solution.py:14
  197.3 36.1 %collective-permute-start.1 = (f32[2,4096]{1,0:T(2,128)}, f32[2,4096]{1,0:T(2,128)S(1)}, u32[]{:S(2)}, u32[]{:S(2)}) collective-permute-start(f32[2,4096]{1,0:T(2,128)} %get-tuple-element.2214), channel_id=1, source_target_pairs={{32,0},{64,32},{96,64},{128,96},{160,128},{192,160},{224,192},{33,... | collective-permute-start | bytes 98312 | tf_op jit(solution)/shard_map/while/body/eval_jaxpr/ppermute | solution.py:14
  407.1 4.5 collective-permute-start
  409.1 5.4 collective-permute-start.1
  561.8 63.1 %copy-start = (s32[8,4096]{1,0:T(8,128)S(1)}, s32[8,4096]{1,0:T(8,128)}, u32[]{:S(2)}) copy-start(s32[8,4096]{1,0:T(8,128)} %get-tuple-element.2247) | copy-start | bytes 393220 | tf_op jit(solution)/shard_map/while
  561.8 63.0 %collective-permute-start = (f32[2,4096]{1,0:T(2,128)}, f32[2,4096]{1,0:T(2,128)S(1)}, u32[]{:S(2)}, u32[]{:S(2)}) collective-permute-start(f32[2,4096]{1,0:T(2,128)} %get-tuple-element.2213), channel_id=1, source_target_pairs={{0,32},{32,64},{64,96},{96,128},{128,160},{160,192},{192,224},{1,3... | collective-permute-start | bytes 98312 | tf_op jit(solution)/shard_map/while/body/eval_jaxpr/ppermute | solution.py:14
  622.9 5.4 collective-permute-start.1
  775.9 31.4 %copy-start = (s32[8,4096]{1,0:T(8,128)S(1)}, s32[8,4096]{1,0:T(8,128)}, u32[]{:S(2)}) copy-start(s32[8,4096]{1,0:T(8,128)} %get-tuple-element.2247) | copy-start | bytes 393220 | tf_op jit(solution)/shard_map/while
  775.9 31.3 %collective-permute-start = (f32[2,4096]{1,0:T(2,128)}, f32[2,4096]{1,0:T(2,128)S(1)}, u32[]{:S(2)}, u32[]{:S(2)}) collective-permute-start(f32[2,4096]{1,0:T(2,128)} %get-tuple-element.2213), channel_id=1, source_target_pairs={{0,32},{32,64},{64,96},{96,128},{128,160},{160,192},{192,224},{1,3... | collective-permute-start | bytes 98312 | tf_op jit(solution)/shard_map/while/body/eval_jaxpr/ppermute | solution.py:14
  805.3 6.5 collective-permute-start.1
  959.1 37.8 %copy-start = (s32[8,4096]{1,0:T(8,128)S(1)}, s32[8,4096]{1,0:T(8,128)}, u32[]{:S(2)}) copy-start(s32[8,4096]{1,0:T(8,128)} %get-tuple-element.2247) | copy-start | bytes 393220 | tf_op jit(solution)/shard_map/while
  959.1 37.7 %collective-permute-start = (f32[2,4096]{1,0:T(2,128)}, f32[2,4096]{1,0:T(2,128)S(1)}, u32[]{:S(2)}, u32[]{:S(2)}) collective-permute-start(f32[2,4096]{1,0:T(2,128)} %get-tuple-element.2213), channel_id=1, source_target_pairs={{0,32},{32,64},{64,96},{96,128},{128,160},{160,192},{192,224},{1,3... | collective-permute-start | bytes 98312 | tf_op jit(solution)/shard_map/while/body/eval_jaxpr/ppermute | solution.py:14
  994.9 11.1 collective-permute-start.1
  1152.9 89.8 %copy-start = (s32[8,4096]{1,0:T(8,128)S(1)}, s32[8,4096]{1,0:T(8,128)}, u32[]{:S(2)}) copy-start(s32[8,4096]{1,0:T(8,128)} %get-tuple-element.2247) | copy-start | bytes 393220 | tf_op jit(solution)/shard_map/while
  1152.9 89.7 %collective-permute-start = (f32[2,4096]{1,0:T(2,128)}, f32[2,4096]{1,0:T(2,128)S(1)}, u32[]{:S(2)}, u32[]{:S(2)}) collective-permute-start(f32[2,4096]{1,0:T(2,128)} %get-tuple-element.2213), channel_id=1, source_target_pairs={{0,32},{32,64},{64,96},{96,128},{128,160},{160,192},{192,224},{1,3... | collective-permute-start | bytes 98312 | tf_op jit(solution)/shard_map/while/body/eval_jaxpr/ppermute | solution.py:14
  1240.7 5.4 collective-permute-start.1
  1425.5 4.5 collective-permute-start
  1427.6 5.4 collective-permute-start.1
  1596.2 12.9 copy-start.1
  1625.1 12.9 copy-start.1
  (5 other events, 11.2 us)
